TPU v7x, 512 devices: a whole 4x4x16 slice. The times are simulated.
512 devices in a mesh: bl: 32 (over y, x, core), dir: 16 (over z).
Axes of the slice: x: 4, y: 4, z: 16, core: 2. Of those that a mesh axis runs over, the one named last changes fastest.
Arguments:
- visibilities: float32 [8, 16, 8192], P(None, 'dir', 'bl'), may hold values from -24 to 24
- coherencies: bfloat16 [32, 8, 16, 8192], P('dir', None, None, 'bl'), may hold values from -6 to 6
- gain_offsets: float32 [32, 8, 512], P(None, None, 'bl'), may hold values from -1.5 to 1.5
- stations: int32 [2, 8192], P(None, 'bl'), may hold values from 0 to 511, as said below
- solve_order: int32 [32], replicated, may hold values from 0 to 31, each once
- counts: int32 [32], replicated, may hold values from 1 to 2
- damping: int32 [32], replicated, may hold values from 1 to 8
Outputs:
- gains: float32 [32, 8, 512], P(None, None, 'bl')
- residual: float32 [8, 16, 8192], P(None, 'dir', 'bl')
Inputs may be any that keep to these rules, and one draw needn't show every extreme that they name: Each baseline names two different stations. `solve_order`: each direction appears once.
All inputs are finite; a program needn't handle non-finite values.
Results may differ from a plain program's by a relative error of at most 0.0003.
Values may be sent and summed in bfloat16 or wider, within the bound.
A program may use at most 64 MiB of HBM per device.

v0:
```python
import jax
import jax.numpy as jnp
from jax import lax
from jax.sharding import PartitionSpec as P

LM_ITERS = 2
SOLVED = 4


def from_root(shard, axis, root):
    mine = lax.axis_index(axis) == root
    return lax.psum(jnp.where(mine, shard, jnp.zeros_like(shard)), axis)


def matrix_entry(mat, i, j):
    return (mat[4 * i + 2 * j], mat[4 * i + 2 * j + 1])


def matmul_two(left, right):
    pieces = []
    for i in (0, 1):
        for j in (0, 1):
            left_r0, left_i0 = matrix_entry(left, i, 0)
            left_r1, left_i1 = matrix_entry(left, i, 1)
            right_r0, right_i0 = matrix_entry(right, 0, j)
            right_r1, right_i1 = matrix_entry(right, 1, j)
            pieces.append(
                left_r0 * right_r0 - left_i0 * right_i0 + left_r1 * right_r1 - left_i1 * right_i1
            )
            pieces.append(
                left_r0 * right_i0 + left_i0 * right_r0 + left_r1 * right_i1 + left_i1 * right_r1
            )
    return jnp.stack(pieces)


def adjoint(mat):
    return jnp.stack([mat[0], -mat[1], mat[4], -mat[5], mat[2], -mat[3], mat[6], -mat[7]])


def apply_gains(gain_p, coher_now, gain_q):
    return matmul_two(matmul_two(gain_p, coher_now), adjoint(gain_q))


def gram_parts(gram):
    return jnp.stack([gram[0], gram[6], gram[2], gram[3]])


def station_terms(gain_p, gain_q, coher_now, target):
    z_rows = matmul_two(coher_now, adjoint(gain_q))
    y_rows = matmul_two(adjoint(coher_now), adjoint(gain_p))
    leading_endpoint = jnp.concatenate(
        [matmul_two(target, adjoint(z_rows)), gram_parts(matmul_two(z_rows, adjoint(z_rows)))], 0
    )
    second = jnp.concatenate(
        [
            matmul_two(adjoint(target), adjoint(y_rows)),
            gram_parts(matmul_two(y_rows, adjoint(y_rows))),
        ],
        0,
    )
    return (jnp.sum(leading_endpoint, axis=1), jnp.sum(second, axis=1))


def solve_station(gathered_sums, gain_now, damp_value):
    numerator = gathered_sums[:8] + damp_value * gain_now
    diag_a = gathered_sums[8] + damp_value
    diag_d = gathered_sums[9] + damp_value
    cross_r = gathered_sums[10]
    cross_i = gathered_sums[11]
    determinant = diag_a * diag_d - cross_r * cross_r - cross_i * cross_i
    zeros_row = jnp.zeros_like(determinant)
    inverse = (
        jnp.stack([diag_d, zeros_row, -cross_r, -cross_i, -cross_r, cross_i, diag_a, zeros_row])
        / determinant
    )
    return matmul_two(numerator, inverse)


def on_device(visibilities, coherencies, gain_offsets, stations, solve_order, counts, damping):
    identity = jnp.zeros((8,), jnp.float32).at[0].set(1.0).at[6].set(1.0)
    start = lax.all_gather(gain_offsets, "bl", axis=2, tiled=True) + identity[None, :, None]
    groups = lax.axis_size("bl")
    channels = visibilities.shape[1]
    total_channels = coherencies.shape[2]
    owned_count = coherencies.shape[0]
    station_count = start.shape[2]
    damping_factor = visibilities.shape[2] * groups * total_channels / station_count
    lane_index = lax.axis_index("dir")
    ends_p = jnp.take(start, stations[0], axis=2)
    ends_q = jnp.take(start, stations[1], axis=2)
    owned_p = lax.dynamic_slice_in_dim(ends_p, lane_index * owned_count, owned_count, 0)
    owned_q = lax.dynamic_slice_in_dim(ends_q, lane_index * owned_count, owned_count, 0)
    gain_p = jnp.transpose(owned_p, (1, 0, 2))[:, :, None, :]
    gain_q = jnp.transpose(owned_q, (1, 0, 2))[:, :, None, :]
    coher_owned = jnp.transpose(coherencies, (1, 0, 2, 3)).astype(jnp.float32)
    partial_value = jnp.sum(apply_gains(gain_p, coher_owned, gain_q), axis=1)
    first_model = lax.psum_scatter(partial_value, "dir", scatter_dimension=1, tiled=True)
    first_residual = visibilities - first_model

    def direction_model(gain_now, coher_now):
        gain_p = jnp.take(gain_now, stations[0], axis=1)[:, None, :]
        gain_q = jnp.take(gain_now, stations[1], axis=1)[:, None, :]
        return apply_gains(gain_p, coher_now, gain_q)

    def sweep(step_index, state):
        gain_table, residual = state
        which = solve_order[step_index]
        owner_row = lax.dynamic_index_in_dim(coherencies, which % owned_count, 0, keepdims=False)
        broadcast_rows = from_root(owner_row, "dir", which // owned_count)
        coher_now = lax.dynamic_slice_in_dim(
            broadcast_rows, lane_index * channels, channels, 1
        ).astype(jnp.float32)
        damp_value = damping[which].astype(jnp.float32) * damping_factor
        gain_start = gain_table[which]
        target = residual + direction_model(gain_start, coher_now)

        def iterate(round_index, gain_now):
            gain_p = jnp.take(gain_now, stations[0], axis=1)[:, None, :]
            gain_q = jnp.take(gain_now, stations[1], axis=1)[:, None, :]
            leading_endpoint, second = station_terms(gain_p, gain_q, coher_now, target)
            local_sums = (
                jax.ops.segment_sum(leading_endpoint.T, stations[0], station_count)
                + jax.ops.segment_sum(second.T, stations[1], station_count)
            ).T
            gathered_sums = lax.psum(local_sums, ("bl", "dir"))
            updated = solve_station(gathered_sums, gain_now, damp_value)
            return jnp.where(round_index < counts[which], updated, gain_now)

        gain_final = lax.fori_loop(0, LM_ITERS, iterate, gain_start)
        residual = target - direction_model(gain_final, coher_now)
        return (gain_table.at[which].set(gain_final), residual)

    gain_table, residual = lax.fori_loop(0, SOLVED, sweep, (start, first_residual))
    own_width = station_count // groups
    gains = lax.dynamic_slice_in_dim(gain_table, lax.axis_index("bl") * own_width, own_width, 2)
    return (gains, residual)


def solution(mesh):
    return jax.shard_map(
        on_device,
        mesh=mesh,
        in_specs=(
            P(None, "dir", "bl"),
            P("dir", None, None, "bl"),
            P(None, None, "bl"),
            P(None, "bl"),
            P(),
            P(),
            P(),
        ),
        out_specs=(P(None, None, "bl"), P(None, "dir", "bl")),
        check_vma=False,
    )
```

profile of v0, /device:TPU:1, one launch (start us, length us, event | category | flops | bytes accessed | tf_op | source)
XLA Modules:
  0.0 1577.4 jit_solution(7976615437648332978)
XLA Ops:
  9.8 29.8 %all_gather.3 = f32[32,8,512]{0,1,2:T(8,128)S(1)} all-gather(f32[32,8,16]{0,1,2:T(8,128)S(1)} %copy.1403), channel_id=1, replica_groups=mesh['bl'=32,'dir'=16] {'bl'}, dimensions={2}, use_global_device_ids=true | all-gather | bytes 540672 | tf_op jit(solution)/shard_map/all_gather | solution.py:81
  40.5 1.0 gather_fusion.7
  41.5 1.1 copy.1408
  44.2 1.0 gather_fusion.6
  48.5 7.5 copy.1415
  56.0 49.5 %reduce-scatter.2.cloned.1.call-done = f32[8,1,256]{2,0,1:T(8,128)} async-done(((f32[8,16,256]{2,0,1:T(8,128)}), f32[8,1,256]{2,0,1:T(8,128)}) %reduce-scatter.2.cloned.1.call-update) | async-done | bytes 8208 | tf_op jit(solution)/shard_map/reduce_scatter | solution.py:97
  106.3 1457.3 %while.54 = (s32[]{:T(128)}, f32[32,8,512]{1,2,0:T(8,128)}, f32[8,1,256]{2,1,0:T(1,128)S(1)}, s32[32]{0:T(128)S(1)}, bf16[2,8,16,256]{3,2,1,0:T(8,128)(2,1)S(1)}...) while((s32[]{:T(128)}, f32[32,8,512]{1,2,0:T(8,128)}, ...), condition=%wide.region_10.13_spmd, body=%wide.region_2.12_spmd.sunk | while | flops 323119 | bytes 2925989 | solution.py:133
  113.5 1.0 dynamic-slice_bitcast_fusion.4
  116.9 125.3 %all-reduce.2.cloned.1.call-done = bf16[8,16,256]{2,1,0:T(8,128)(2,1)} async-done(((bf16[8,16,256]{2,1,0:T(8,128)(2,1)}), bf16[8,16,256]{2,1,0:T(8,128)(2,1)}) %all-reduce.2.cloned.1.call-update) | async-done | bytes 65552 | tf_op jit(solution)/shard_map/while/body/eval_jaxpr/psum | solution.py:12
  243.2 235.5 %while.55 = (s32[]{:T(128)}, f32[8,512]{0,1:T(8,128)S(1)}, s32[1]{0:T(128)}, s32[2,256]{1,0:T(2,128)S(1)}, f32[8,1,256]{2,1,0:T(1,128)S(1)}, /*index=5*/f32[8,1,...) while((s32[]{:T(128)}, f32[8,512]{0,1:T(8,128)S(1)}, ...), condition=%wide.region_9.11_spmd, body=%wide.region_5.10_spmd.sunk | while | flops 164865 | bytes 1329347 | solution.py:129
  246.4 1.5 scatter_custom_fusion.10
  247.9 1.5 scatter_custom_fusion.11
  249.5 112.0 %psum.29 = f32[12,512]{0,1:T(8,128)S(1)} all-reduce(f32[12,512]{0,1:T(8,128)S(1)} %add_bitcast_fusion.2), channel_id=1, replica_groups=mesh['bl'=32,'dir'=16] {'bl','dir'}, use_global_device_ids=true, to_apply=%region_8.9 | all-reduce | flops 6144 | bytes 49152 | tf_op jit(solution)/shard_map/while/body/eval_jaxpr/while/body/eval_jaxpr/psum | solution.py:125
  369.5 1.5 scatter_custom_fusion.10
  371.0 1.5 scatter_custom_fusion.11
  372.5 101.4 %psum.29 = f32[12,512]{0,1:T(8,128)S(1)} all-reduce(f32[12,512]{0,1:T(8,128)S(1)} %add_bitcast_fusion.2), channel_id=1, replica_groups=mesh['bl'=32,'dir'=16] {'bl','dir'}, use_global_device_ids=true, to_apply=%region_8.9 | all-reduce | flops 6144 | bytes 49152 | tf_op jit(solution)/shard_map/while/body/eval_jaxpr/while/body/eval_jaxpr/psum | solution.py:125
  480.5 2.3 fusion.153
  490.0 1.0 dynamic-slice_bitcast_fusion.4
  493.4 109.1 %all-reduce.2.cloned.1.call-done = bf16[8,16,256]{2,1,0:T(8,128)(2,1)} async-done(((bf16[8,16,256]{2,1,0:T(8,128)(2,1)}), bf16[8,16,256]{2,1,0:T(8,128)(2,1)}) %all-reduce.2.cloned.1.call-update) | async-done | bytes 65552 | tf_op jit(solution)/shard_map/while/body/eval_jaxpr/psum | solution.py:12
  603.5 235.5 %while.55 = (s32[]{:T(128)}, f32[8,512]{0,1:T(8,128)S(1)}, s32[1]{0:T(128)}, s32[2,256]{1,0:T(2,128)S(1)}, f32[8,1,256]{2,1,0:T(1,128)S(1)}, /*index=5*/f32[8,1,...) while((s32[]{:T(128)}, f32[8,512]{0,1:T(8,128)S(1)}, ...), condition=%wide.region_9.11_spmd, body=%wide.region_5.10_spmd.sunk | while | flops 164865 | bytes 1329347 | solution.py:129
  606.7 1.5 scatter_custom_fusion.10
  608.2 1.5 scatter_custom_fusion.11
  609.7 112.0 %psum.29 = f32[12,512]{0,1:T(8,128)S(1)} all-reduce(f32[12,512]{0,1:T(8,128)S(1)} %add_bitcast_fusion.2), channel_id=1, replica_groups=mesh['bl'=32,'dir'=16] {'bl','dir'}, use_global_device_ids=true, to_apply=%region_8.9 | all-reduce | flops 6144 | bytes 49152 | tf_op jit(solution)/shard_map/while/body/eval_jaxpr/while/body/eval_jaxpr/psum | solution.py:125
  729.7 1.5 scatter_custom_fusion.10
  731.2 1.5 scatter_custom_fusion.11
  732.8 101.4 %psum.29 = f32[12,512]{0,1:T(8,128)S(1)} all-reduce(f32[12,512]{0,1:T(8,128)S(1)} %add_bitcast_fusion.2), channel_id=1, replica_groups=mesh['bl'=32,'dir'=16] {'bl','dir'}, use_global_device_ids=true, to_apply=%region_8.9 | all-reduce | flops 6144 | bytes 49152 | tf_op jit(solution)/shard_map/while/body/eval_jaxpr/while/body/eval_jaxpr/psum | solution.py:125
  840.8 2.3 fusion.153
  850.2 1.0 dynamic-slice_bitcast_fusion.4
  853.6 109.1 %all-reduce.2.cloned.1.call-done = bf16[8,16,256]{2,1,0:T(8,128)(2,1)} async-done(((bf16[8,16,256]{2,1,0:T(8,128)(2,1)}), bf16[8,16,256]{2,1,0:T(8,128)(2,1)}) %all-reduce.2.cloned.1.call-update) | async-done | bytes 65552 | tf_op jit(solution)/shard_map/while/body/eval_jaxpr/psum | solution.py:12
  963.7 235.5 %while.55 = (s32[]{:T(128)}, f32[8,512]{0,1:T(8,128)S(1)}, s32[1]{0:T(128)}, s32[2,256]{1,0:T(2,128)S(1)}, f32[8,1,256]{2,1,0:T(1,128)S(1)}, /*index=5*/f32[8,1,...) while((s32[]{:T(128)}, f32[8,512]{0,1:T(8,128)S(1)}, ...), condition=%wide.region_9.11_spmd, body=%wide.region_5.10_spmd.sunk | while | flops 164865 | bytes 1329347 | solution.py:129
  966.9 1.5 scatter_custom_fusion.10
  968.4 1.5 scatter_custom_fusion.11
  970.0 112.0 %psum.29 = f32[12,512]{0,1:T(8,128)S(1)} all-reduce(f32[12,512]{0,1:T(8,128)S(1)} %add_bitcast_fusion.2), channel_id=1, replica_groups=mesh['bl'=32,'dir'=16] {'bl','dir'}, use_global_device_ids=true, to_apply=%region_8.9 | all-reduce | flops 6144 | bytes 49152 | tf_op jit(solution)/shard_map/while/body/eval_jaxpr/while/body/eval_jaxpr/psum | solution.py:125
  1090.0 1.5 scatter_custom_fusion.10
  1091.5 1.5 scatter_custom_fusion.11
  1093.0 101.4 %psum.29 = f32[12,512]{0,1:T(8,128)S(1)} all-reduce(f32[12,512]{0,1:T(8,128)S(1)} %add_bitcast_fusion.2), channel_id=1, replica_groups=mesh['bl'=32,'dir'=16] {'bl','dir'}, use_global_device_ids=true, to_apply=%region_8.9 | all-reduce | flops 6144 | bytes 49152 | tf_op jit(solution)/shard_map/while/body/eval_jaxpr/while/body/eval_jaxpr/psum | solution.py:125
  1201.0 2.3 fusion.153
  1210.5 1.0 dynamic-slice_bitcast_fusion.4
  1213.9 109.1 %all-reduce.2.cloned.1.call-done = bf16[8,16,256]{2,1,0:T(8,128)(2,1)} async-done(((bf16[8,16,256]{2,1,0:T(8,128)(2,1)}), bf16[8,16,256]{2,1,0:T(8,128)(2,1)}) %all-reduce.2.cloned.1.call-update) | async-done | bytes 65552 | tf_op jit(solution)/shard_map/while/body/eval_jaxpr/psum | solution.py:12
  1324.0 235.5 %while.55 = (s32[]{:T(128)}, f32[8,512]{0,1:T(8,128)S(1)}, s32[1]{0:T(128)}, s32[2,256]{1,0:T(2,128)S(1)}, f32[8,1,256]{2,1,0:T(1,128)S(1)}, /*index=5*/f32[8,1,...) while((s32[]{:T(128)}, f32[8,512]{0,1:T(8,128)S(1)}, ...), condition=%wide.region_9.11_spmd, body=%wide.region_5.10_spmd.sunk | while | flops 164865 | bytes 1329347 | solution.py:129
  1327.2 1.5 scatter_custom_fusion.10
  1328.7 1.5 scatter_custom_fusion.11
  1330.2 112.0 %psum.29 = f32[12,512]{0,1:T(8,128)S(1)} all-reduce(f32[12,512]{0,1:T(8,128)S(1)} %add_bitcast_fusion.2), channel_id=1, replica_groups=mesh['bl'=32,'dir'=16] {'bl','dir'}, use_global_device_ids=true, to_apply=%region_8.9 | all-reduce | flops 6144 | bytes 49152 | tf_op jit(solution)/shard_map/while/body/eval_jaxpr/while/body/eval_jaxpr/psum | solution.py:125
  1450.2 1.5 scatter_custom_fusion.10
  1451.7 1.5 scatter_custom_fusion.11
  1453.3 101.4 %psum.29 = f32[12,512]{0,1:T(8,128)S(1)} all-reduce(f32[12,512]{0,1:T(8,128)S(1)} %add_bitcast_fusion.2), channel_id=1, replica_groups=mesh['bl'=32,'dir'=16] {'bl','dir'}, use_global_device_ids=true, to_apply=%region_8.9 | all-reduce | flops 6144 | bytes 49152 | tf_op jit(solution)/shard_map/while/body/eval_jaxpr/while/body/eval_jaxpr/psum | solution.py:125
  1561.2 2.3 fusion.153
  1563.6 6.7 copy.1417
  (770 shorter events, 97.4 us)
Async XLA Ops:
  7.2 98.3 %reduce-scatter.2.cloned.1.call-start = ((), (), s32[]{:S(2)}) async-start(), calls=%async_computation.1 | async-start | bytes 139264 | tf_op jit(solution)/shard_map/reduce_scatter | solution.py:97
  45.5 1.8 copy-start.3
  45.6 1.8 copy-start.4
  45.6 1.8 copy-start.5
  45.6 1.8 copy-start.6
  48.4 57.1 %copy-start.8 = (f32[8,1,256]{2,1,0:T(1,128)S(1)}, f32[8,1,256]{2,1,0:T(1,128)}, u32[]{:S(2)}) copy-start(f32[8,1,256]{2,1,0:T(1,128)} %param.21) | copy-start | bytes 24580
  48.4 57.8 %copy-start = (s32[2,256]{1,0:T(2,128)S(1)}, s32[2,256]{1,0:T(2,128)}, u32[]{:S(2)}) copy-start(s32[2,256]{1,0:T(2,128)} %param.24) | copy-start | bytes 6148
  48.4 57.8 %copy-start.1 = (bf16[2,8,16,256]{3,2,1,0:T(8,128)(2,1)S(1)}, bf16[2,8,16,256]{3,2,1,0:T(8,128)(2,1)}, u32[]{:S(2)}) copy-start(bf16[2,8,16,256]{3,2,1,0:T(8,128)(2,1)} %param.22) | copy-start | bytes 393220
  48.4 57.8 %copy-start.7 = (s32[3]{0:T(128)S(1)}, s32[3]{0:T(128)}, u32[]{:S(2)}) copy-start(s32[3]{0:T(128)} %constant.291.clone.1) | copy-start | bytes 40
  48.4 57.8 %copy-start.9 = (s32[32]{0:T(128)S(1)}, s32[32]{0:T(128)}, u32[]{:S(2)}) copy-start(s32[32]{0:T(128)} %param.25) | copy-start | bytes 388
  48.5 57.8 %copy-start.10 = (s32[32]{0:T(128)S(1)}, s32[32]{0:T(128)}, u32[]{:S(2)}) copy-start(s32[32]{0:T(128)} %param.27) | copy-start | bytes 388
  48.5 57.8 %copy-start.11 = (s32[32]{0:T(128)S(1)}, s32[32]{0:T(128)}, u32[]{:S(2)}) copy-start(s32[32]{0:T(128)} %param.26) | copy-start | bytes 388
  106.3 135.9 %all-reduce.2.cloned.1.call-start = ((), (), s32[]{:S(2)}) async-start(), calls=%async_computation.2 | async-start | bytes 131072 | tf_op jit(solution)/shard_map/while/body/eval_jaxpr/psum | solution.py:12
  482.8 119.7 %all-reduce.2.cloned.1.call-start = ((), (), s32[]{:S(2)}) async-start(), calls=%async_computation.2 | async-start | bytes 131072 | tf_op jit(solution)/shard_map/while/body/eval_jaxpr/psum | solution.py:12
  843.1 119.7 %all-reduce.2.cloned.1.call-start = ((), (), s32[]{:S(2)}) async-start(), calls=%async_computation.2 | async-start | bytes 131072 | tf_op jit(solution)/shard_map/while/body/eval_jaxpr/psum | solution.py:12
  1203.3 119.7 %all-reduce.2.cloned.1.call-start = ((), (), s32[]{:S(2)}) async-start(), calls=%async_computation.2 | async-start | bytes 131072 | tf_op jit(solution)/shard_map/while/body/eval_jaxpr/psum | solution.py:12
  1563.6 6.7 copy-start.2
Sparse Core Ops, SparseCore 0:
  48.5 56.9 reduce-scatter.1
  110.4 131.8 all-reduce.1
  486.8 115.5 all-reduce.1
  847.1 115.5 all-reduce.1
  1207.3 115.5 all-reduce.1
where the time goes:
time: 1580 us
  blocking collectives  884 us (56%)
  waiting for transfers between devices  502 us (32%)
  local copies, waits for them, and re-layouts  93.9 us (6%)
  other arithmetic  57.8 us (4%)
  loops' own time  25.7 us (2%)
    psum x8, blocking collectives, iterate(): gathered_sums = lax.psum(local_sums, ('bl', 'dir'))  854 us
    psum x4, waiting for transfers between devices, from_root(): return lax.psum(jnp.where(mine, shard, jnp.zeros_like(shard)), axis)  453 us
    reduce_scatter x1, waiting for transfers between devices, on_device(): lax.psum_scatter(partial_value, 'dir', scatter_dimension=1, tiled=True)  49.5 us
  transfers between devices with their start and end apart: 5, of which 5 were waited for; matrix products, arithmetic and copies ran while one was open for 2% of the time, Pallas kernels for 0%

commit v1 on v0

--- a/solution.py
+++ b/solution.py
@@ -122,7 +122,7 @@
                 jax.ops.segment_sum(leading_endpoint.T, stations[0], station_count)
                 + jax.ops.segment_sum(second.T, stations[1], station_count)
             ).T
-            gathered_sums = lax.psum(local_sums, ("bl", "dir"))
+            gathered_sums = jnp.sum(lax.all_gather(local_sums, ("bl", "dir")), axis=0)
             updated = solve_station(gathered_sums, gain_now, damp_value)
             return jnp.where(round_index < counts[which], updated, gain_now)
 

time: 1580 us -> 2520 us (1.59)
  waiting for transfers between devices: 502 us -> 2270 us
  blocking collectives: 884 us -> 29.8 us
  other arithmetic: 57.8 us -> 107 us
    all_gather x0 -> x8, waiting for transfers between devices: none -> 1760 us  [iterate(): gathered_sums = jnp.sum(lax.all_gather(local_sums, ('bl', 'dir')), axis=0)]
    psum x8 -> x0, blocking collectives: 854 us -> none  [iterate(): gathered_sums = lax.psum(local_sums, ('bl', 'dir'))]
    reduce_sum x0 -> x8, other arithmetic: none -> 53.9 us  [iterate(): gathered_sums = jnp.sum(lax.all_gather(local_sums, ('bl', 'dir')), axis=0)]
  transfers between devices with their start and end apart: 5 -> 13, of which waited for: 5 -> 13; matrix products, arithmetic and copies ran while one was open for 2% -> 1% of each run, Pallas kernels for 0% -> 0%
where the time goes in v1:
time: 2520 us
  waiting for transfers between devices  2270 us (90%)
  other arithmetic  107 us (4%)
  local copies, waits for them, and re-layouts  69 us (3%)
  blocking collectives  29.8 us (1%)
  loops' own time  25.5 us (1%)
    all_gather x8, waiting for transfers between devices, iterate(): gathered_sums = jnp.sum(lax.all_gather(local_sums, ('bl', 'dir')), axis=0)  1760 us
    psum x4, waiting for transfers between devices, from_root(): return lax.psum(jnp.where(mine, shard, jnp.zeros_like(shard)), axis)  459 us
    reduce_sum x8, other arithmetic, iterate(): gathered_sums = jnp.sum(lax.all_gather(local_sums, ('bl', 'dir')), axis=0)  53.9 us
  transfers between devices with their start and end apart: 13, of which 13 were waited for; matrix products, arithmetic and copies ran while one was open for 1% of the time, Pallas kernels for 0%

profile of v1, /device:TPU:1, one launch (start us, length us, event | category | flops | bytes accessed | tf_op | source)
XLA Modules:
  0.0 2519.3 jit_solution(11574973723410222921)
XLA Ops:
  9.8 29.8 %all_gather.19 = f32[32,8,512]{0,1,2:T(8,128)S(1)} all-gather(f32[32,8,16]{0,1,2:T(8,128)S(1)} %copy.860), channel_id=1, replica_groups=mesh['bl'=32,'dir'=16] {'bl'}, dimensions={2}, use_global_device_ids=true | all-gather | bytes 540672 | tf_op jit(solution)/shard_map/all_gather | solution.py:81
  48.5 7.4 copy.872
  55.9 49.6 %reduce-scatter.2.cloned.1.call-done = f32[8,1,256]{2,0,1:T(8,128)} async-done(((f32[8,16,256]{2,0,1:T(8,128)}), f32[8,1,256]{2,0,1:T(8,128)}) %reduce-scatter.2.cloned.1.call-update) | async-done | bytes 8208 | tf_op jit(solution)/shard_map/reduce_scatter | solution.py:97
  106.3 2399.1 %while.54 = (s32[]{:T(128)}, f32[32,8,512]{1,2,0:T(8,128)}, f32[8,1,256]{2,1,0:T(1,128)S(1)}, s32[32]{0:T(128)S(1)}, bf16[2,8,16,256]{3,2,1,0:T(8,128)(2,1)S(1)}...) while((s32[]{:T(128)}, f32[32,8,512]{1,2,0:T(8,128)}, ...), condition=%wide.region_10.13_spmd, body=%wide.region_2.12_spmd.sunk | while | flops 3456559 | bytes 57476556 | solution.py:133
  116.8 125.4 %all-reduce.2.cloned.1.call-done = bf16[8,16,256]{2,1,0:T(8,128)(2,1)} async-done(((bf16[8,16,256]{2,1,0:T(8,128)(2,1)}), bf16[8,16,256]{2,1,0:T(8,128)(2,1)}) %all-reduce.2.cloned.1.call-update) | async-done | bytes 65552 | tf_op jit(solution)/shard_map/while/body/eval_jaxpr/psum | solution.py:12
  243.2 469.6 %while.55 = (s32[]{:T(128)}, f32[8,512]{0,1:T(8,128)S(1)}, s32[1]{0:T(128)}, s32[2,256]{1,0:T(2,128)S(1)}, f32[8,1,256]{2,1,0:T(1,128)S(1)}, /*index=5*/f32[8,1,...) while((s32[]{:T(128)}, f32[8,512]{0,1:T(8,128)S(1)}, ...), condition=%wide.region_9.11_spmd, body=%wide.region_5.10_spmd.sunk | while | flops 3298305 | bytes 55879916 | solution.py:129
  245.7 1.5 scatter_custom_fusion.10
  247.2 1.5 scatter_custom_fusion.11
  250.2 226.5 %all-gather.6.cloned.1.call-done = f32[512,12,512]{2,1,0:T(8,128)} async-done(((f32[1,12,512]{2,1,0:T(8,128)}), f32[512,12,512]{2,1,0:T(8,128)}) %all-gather.6.cloned.1.call-update) | async-done | bytes 12582928 | tf_op jit(solution)/shard_map/while/body/eval_jaxpr/while/body/eval_jaxpr/all_gather | solution.py:125
  476.7 6.7 reduce_sum.41
  486.3 1.5 scatter_custom_fusion.10
  487.8 1.5 scatter_custom_fusion.11
  490.9 214.8 %all-gather.6.cloned.1.call-done = f32[512,12,512]{2,1,0:T(8,128)} async-done(((f32[1,12,512]{2,1,0:T(8,128)}), f32[512,12,512]{2,1,0:T(8,128)}) %all-gather.6.cloned.1.call-update) | async-done | bytes 12582928 | tf_op jit(solution)/shard_map/while/body/eval_jaxpr/while/body/eval_jaxpr/all_gather | solution.py:125
  705.6 6.7 reduce_sum.41
  714.6 2.3 fusion.149
  727.3 111.0 %all-reduce.2.cloned.1.call-done = bf16[8,16,256]{2,1,0:T(8,128)(2,1)} async-done(((bf16[8,16,256]{2,1,0:T(8,128)(2,1)}), bf16[8,16,256]{2,1,0:T(8,128)(2,1)}) %all-reduce.2.cloned.1.call-update) | async-done | bytes 65552 | tf_op jit(solution)/shard_map/while/body/eval_jaxpr/psum | solution.py:12
  839.4 469.6 %while.55 = (s32[]{:T(128)}, f32[8,512]{0,1:T(8,128)S(1)}, s32[1]{0:T(128)}, s32[2,256]{1,0:T(2,128)S(1)}, f32[8,1,256]{2,1,0:T(1,128)S(1)}, /*index=5*/f32[8,1,...) while((s32[]{:T(128)}, f32[8,512]{0,1:T(8,128)S(1)}, ...), condition=%wide.region_9.11_spmd, body=%wide.region_5.10_spmd.sunk | while | flops 3298305 | bytes 55879916 | solution.py:129
  841.8 1.5 scatter_custom_fusion.10
  843.3 1.5 scatter_custom_fusion.11
  846.4 226.5 %all-gather.6.cloned.1.call-done = f32[512,12,512]{2,1,0:T(8,128)} async-done(((f32[1,12,512]{2,1,0:T(8,128)}), f32[512,12,512]{2,1,0:T(8,128)}) %all-gather.6.cloned.1.call-update) | async-done | bytes 12582928 | tf_op jit(solution)/shard_map/while/body/eval_jaxpr/while/body/eval_jaxpr/all_gather | solution.py:125
  1072.9 6.7 reduce_sum.41
  1082.5 1.5 scatter_custom_fusion.10
  1084.0 1.5 scatter_custom_fusion.11
  1087.0 214.8 %all-gather.6.cloned.1.call-done = f32[512,12,512]{2,1,0:T(8,128)} async-done(((f32[1,12,512]{2,1,0:T(8,128)}), f32[512,12,512]{2,1,0:T(8,128)}) %all-gather.6.cloned.1.call-update) | async-done | bytes 12582928 | tf_op jit(solution)/shard_map/while/body/eval_jaxpr/while/body/eval_jaxpr/all_gather | solution.py:125
  1301.8 6.7 reduce_sum.41
  1310.8 2.3 fusion.149
  1323.5 111.0 %all-reduce.2.cloned.1.call-done = bf16[8,16,256]{2,1,0:T(8,128)(2,1)} async-done(((bf16[8,16,256]{2,1,0:T(8,128)(2,1)}), bf16[8,16,256]{2,1,0:T(8,128)(2,1)}) %all-reduce.2.cloned.1.call-update) | async-done | bytes 65552 | tf_op jit(solution)/shard_map/while/body/eval_jaxpr/psum | solution.py:12
  1435.5 469.6 %while.55 = (s32[]{:T(128)}, f32[8,512]{0,1:T(8,128)S(1)}, s32[1]{0:T(128)}, s32[2,256]{1,0:T(2,128)S(1)}, f32[8,1,256]{2,1,0:T(1,128)S(1)}, /*index=5*/f32[8,1,...) while((s32[]{:T(128)}, f32[8,512]{0,1:T(8,128)S(1)}, ...), condition=%wide.region_9.11_spmd, body=%wide.region_5.10_spmd.sunk | while | flops 3298305 | bytes 55879916 | solution.py:129
  1438.0 1.5 scatter_custom_fusion.10
  1439.5 1.5 scatter_custom_fusion.11
  1442.5 226.5 %all-gather.6.cloned.1.call-done = f32[512,12,512]{2,1,0:T(8,128)} async-done(((f32[1,12,512]{2,1,0:T(8,128)}), f32[512,12,512]{2,1,0:T(8,128)}) %all-gather.6.cloned.1.call-update) | async-done | bytes 12582928 | tf_op jit(solution)/shard_map/while/body/eval_jaxpr/while/body/eval_jaxpr/all_gather | solution.py:125
  1669.0 6.7 reduce_sum.41
  1678.7 1.5 scatter_custom_fusion.10
  1680.2 1.5 scatter_custom_fusion.11
  1683.2 214.8 %all-gather.6.cloned.1.call-done = f32[512,12,512]{2,1,0:T(8,128)} async-done(((f32[1,12,512]{2,1,0:T(8,128)}), f32[512,12,512]{2,1,0:T(8,128)}) %all-gather.6.cloned.1.call-update) | async-done | bytes 12582928 | tf_op jit(solution)/shard_map/while/body/eval_jaxpr/while/body/eval_jaxpr/all_gather | solution.py:125
  1898.0 6.7 reduce_sum.41
  1906.9 2.3 fusion.149
  1919.7 111.0 %all-reduce.2.cloned.1.call-done = bf16[8,16,256]{2,1,0:T(8,128)(2,1)} async-done(((bf16[8,16,256]{2,1,0:T(8,128)(2,1)}), bf16[8,16,256]{2,1,0:T(8,128)(2,1)}) %all-reduce.2.cloned.1.call-update) | async-done | bytes 65552 | tf_op jit(solution)/shard_map/while/body/eval_jaxpr/psum | solution.py:12
  2031.7 469.6 %while.55 = (s32[]{:T(128)}, f32[8,512]{0,1:T(8,128)S(1)}, s32[1]{0:T(128)}, s32[2,256]{1,0:T(2,128)S(1)}, f32[8,1,256]{2,1,0:T(1,128)S(1)}, /*index=5*/f32[8,1,...) while((s32[]{:T(128)}, f32[8,512]{0,1:T(8,128)S(1)}, ...), condition=%wide.region_9.11_spmd, body=%wide.region_5.10_spmd.sunk | while | flops 3298305 | bytes 55879916 | solution.py:129
  2034.2 1.5 scatter_custom_fusion.10
  2035.7 1.5 scatter_custom_fusion.11
  2038.7 226.5 %all-gather.6.cloned.1.call-done = f32[512,12,512]{2,1,0:T(8,128)} async-done(((f32[1,12,512]{2,1,0:T(8,128)}), f32[512,12,512]{2,1,0:T(8,128)}) %all-gather.6.cloned.1.call-update) | async-done | bytes 12582928 | tf_op jit(solution)/shard_map/while/body/eval_jaxpr/while/body/eval_jaxpr/all_gather | solution.py:125
  2265.2 6.7 reduce_sum.41
  2276.3 1.5 scatter_custom_fusion.11
  2279.4 214.8 %all-gather.6.cloned.1.call-done = f32[512,12,512]{2,1,0:T(8,128)} async-done(((f32[1,12,512]{2,1,0:T(8,128)}), f32[512,12,512]{2,1,0:T(8,128)}) %all-gather.6.cloned.1.call-update) | async-done | bytes 12582928 | tf_op jit(solution)/shard_map/while/body/eval_jaxpr/while/body/eval_jaxpr/all_gather | solution.py:125
  2494.1 6.7 reduce_sum.41
  2503.1 2.3 fusion.149
  2505.4 6.7 copy.874
  (682 shorter events, 77.2 us)
Async XLA Ops:
  7.2 98.3 %reduce-scatter.2.cloned.1.call-start = ((), (), s32[]{:S(2)}) async-start(), calls=%async_computation.1 | async-start | bytes 139264 | tf_op jit(solution)/shard_map/reduce_scatter | solution.py:97
  45.5 1.8 copy-start.3
  45.6 1.8 copy-start.4
  45.6 1.8 copy-start.5
  45.6 1.8 copy-start.6
  48.4 57.1 %copy-start.8 = (f32[8,1,256]{2,1,0:T(1,128)S(1)}, f32[8,1,256]{2,1,0:T(1,128)}, u32[]{:S(2)}) copy-start(f32[8,1,256]{2,1,0:T(1,128)} %param.21) | copy-start | bytes 24580
  48.4 57.8 %copy-start = (s32[2,256]{1,0:T(2,128)S(1)}, s32[2,256]{1,0:T(2,128)}, u32[]{:S(2)}) copy-start(s32[2,256]{1,0:T(2,128)} %param.24) | copy-start | bytes 6148
  48.4 57.8 %copy-start.1 = (bf16[2,8,16,256]{3,2,1,0:T(8,128)(2,1)S(1)}, bf16[2,8,16,256]{3,2,1,0:T(8,128)(2,1)}, u32[]{:S(2)}) copy-start(bf16[2,8,16,256]{3,2,1,0:T(8,128)(2,1)} %param.22) | copy-start | bytes 393220
  48.4 57.8 %copy-start.7 = (s32[3]{0:T(128)S(1)}, s32[3]{0:T(128)}, u32[]{:S(2)}) copy-start(s32[3]{0:T(128)} %constant.291.clone.1) | copy-start | bytes 40
  48.4 57.8 %copy-start.9 = (s32[32]{0:T(128)S(1)}, s32[32]{0:T(128)}, u32[]{:S(2)}) copy-start(s32[32]{0:T(128)} %param.25) | copy-start | bytes 388
  48.5 57.8 %copy-start.10 = (s32[32]{0:T(128)S(1)}, s32[32]{0:T(128)}, u32[]{:S(2)}) copy-start(s32[32]{0:T(128)} %param.27) | copy-start | bytes 388
  48.5 57.8 %copy-start.11 = (s32[32]{0:T(128)S(1)}, s32[32]{0:T(128)}, u32[]{:S(2)}) copy-start(s32[32]{0:T(128)} %param.26) | copy-start | bytes 388
  106.3 135.9 %all-reduce.2.cloned.1.call-start = ((), (), s32[]{:S(2)}) async-start(), calls=%async_computation.2 | async-start | bytes 131072 | tf_op jit(solution)/shard_map/while/body/eval_jaxpr/psum | solution.py:12
  243.2 233.5 %all-gather.6.cloned.1.call-start = ((), (), s32[]{:S(2)}) async-start(), calls=%async_computation.3 | async-start | bytes 16809984 | tf_op jit(solution)/shard_map/while/body/eval_jaxpr/while/body/eval_jaxpr/all_gather | solution.py:125
  483.9 221.8 %all-gather.6.cloned.1.call-start = ((), (), s32[]{:S(2)}) async-start(), calls=%async_computation.3 | async-start | bytes 16809984 | tf_op jit(solution)/shard_map/while/body/eval_jaxpr/while/body/eval_jaxpr/all_gather | solution.py:125
  716.9 121.4 %all-reduce.2.cloned.1.call-start = ((), (), s32[]{:S(2)}) async-start(), calls=%async_computation.2 | async-start | bytes 131072 | tf_op jit(solution)/shard_map/while/body/eval_jaxpr/psum | solution.py:12
  839.4 233.5 %all-gather.6.cloned.1.call-start = ((), (), s32[]{:S(2)}) async-start(), calls=%async_computation.3 | async-start | bytes 16809984 | tf_op jit(solution)/shard_map/while/body/eval_jaxpr/while/body/eval_jaxpr/all_gather | solution.py:125
  1080.0 221.8 %all-gather.6.cloned.1.call-start = ((), (), s32[]{:S(2)}) async-start(), calls=%async_computation.3 | async-start | bytes 16809984 | tf_op jit(solution)/shard_map/while/body/eval_jaxpr/while/body/eval_jaxpr/all_gather | solution.py:125
  1313.1 121.4 %all-reduce.2.cloned.1.call-start = ((), (), s32[]{:S(2)}) async-start(), calls=%async_computation.2 | async-start | bytes 131072 | tf_op jit(solution)/shard_map/while/body/eval_jaxpr/psum | solution.py:12
  1435.5 233.5 %all-gather.6.cloned.1.call-start = ((), (), s32[]{:S(2)}) async-start(), calls=%async_computation.3 | async-start | bytes 16809984 | tf_op jit(solution)/shard_map/while/body/eval_jaxpr/while/body/eval_jaxpr/all_gather | solution.py:125
  1676.2 221.8 %all-gather.6.cloned.1.call-start = ((), (), s32[]{:S(2)}) async-start(), calls=%async_computation.3 | async-start | bytes 16809984 | tf_op jit(solution)/shard_map/while/body/eval_jaxpr/while/body/eval_jaxpr/all_gather | solution.py:125
  1909.3 121.4 %all-reduce.2.cloned.1.call-start = ((), (), s32[]{:S(2)}) async-start(), calls=%async_computation.2 | async-start | bytes 131072 | tf_op jit(solution)/shard_map/while/body/eval_jaxpr/psum | solution.py:12
  2031.7 233.5 %all-gather.6.cloned.1.call-start = ((), (), s32[]{:S(2)}) async-start(), calls=%async_computation.3 | async-start | bytes 16809984 | tf_op jit(solution)/shard_map/while/body/eval_jaxpr/while/body/eval_jaxpr/all_gather | solution.py:125
  2272.4 221.8 %all-gather.6.cloned.1.call-start = ((), (), s32[]{:S(2)}) async-start(), calls=%async_computation.3 | async-start | bytes 16809984 | tf_op jit(solution)/shard_map/while/body/eval_jaxpr/while/body/eval_jaxpr/all_gather | solution.py:125
  2505.4 6.7 copy-start.2
Sparse Core Ops, SparseCore 0:
  48.5 56.9 reduce-scatter.1
  110.3 131.8 all-reduce.1
  249.6 227.0 all-gather.5
  490.3 215.3 all-gather.5
  720.9 117.4 all-reduce.1
  845.8 227.0 all-gather.5
  1086.4 215.3 all-gather.5
  1317.1 117.4 all-reduce.1
  1441.9 227.0 all-gather.5
  1682.6 215.3 all-gather.5
  1913.2 117.4 all-reduce.1
  2038.1 227.0 all-gather.5
  2278.7 215.3 all-gather.5
